TPU v7x, 512 devices: a whole 4x8x8 slice. The times are simulated.
512 devices in a mesh: grp: 4 (over y_lo, core), src: 16 (over y_hi, x), rcv: 8 (over z).
Axes of the slice: x: 4, y: 8 (y_hi: 4, y_lo: 2; y = y_hi * 2 + y_lo), z: 8, core: 2. Of those that a mesh axis runs over, the one named last changes fastest.
Arguments:
- recorded: bfloat16 [4, 2, 4096, 4096], P('grp', None, 'src', 'rcv'), parts along dimension 0, as said below
- aperture: int32 [128, 32, 3], P(('grp', 'src'), 'rcv'), parts along dimension 0, may hold values from 0 to 32, as said below
Outputs:
- multiples: float32 [4, 2, 4096, 4096], P('grp', None, 'src', 'rcv'), parts along dimension 0
There are 4 independent parts, one for each index of `grp`. A program takes and returns all parts, laid end to end along the dimension named above; each array names one. Nothing has to cross between parts.
Inputs may be any that keep to these rules, and one draw needn't show every extreme that they name: The data obey reciprocity: recorded(f, c, q, j) equals recorded(f, c, j, q). `aperture`: field 1 is from 4 to 32, field 0 plus field 1 is at most 32, field 2 is from 0 to 2. In every draw some tile pair spans all 32 k-blocks and some has taper width 2.
All inputs are finite; a program needn't handle non-finite values.
Results may differ from a plain program's by a relative error of at most 0.0004.
Values may be sent and summed in bfloat16 or wider, within the bound.
No kernel may reach another device: no remote copies, remote signals or barrier semaphores. Data moves between devices by JAX's collectives and lax.ppermute only.
A program may use at most 64 MiB of HBM per device.

v0:
```python
import jax
import jax.numpy as jnp
from jax import lax
from jax.sharding import PartitionSpec as P

NB = 32
TILE = 128


def tile_weights(aperture):
    block_ids = jnp.arange(NB, dtype=jnp.int32)
    offset = block_ids[None, None, :] - aperture[..., 0:1]
    extent = aperture[..., 1:2]
    taper_width = aperture[..., 2:3]
    margin = jnp.minimum(offset, extent - 1 - offset)
    ramped = jnp.minimum(
        1.0, (margin + 1).astype(jnp.float32) / (taper_width + 1).astype(jnp.float32)
    )
    return jnp.where((offset >= 0) & (offset < extent), ramped, 0.0)


def shards(recorded, aperture):
    slices = recorded.shape[0]
    own_rows = recorded.shape[2]
    own_cols = recorded.shape[3]
    row_tiles = own_rows // TILE
    col_tiles = own_cols // TILE
    weights = tile_weights(aperture)
    block_ids = jnp.arange(NB, dtype=jnp.int32)
    left_panel = lax.all_gather(recorded, "rcv", axis=3, tiled=True)

    def block_terms(incoming, first_row, span_rows, tile_weight):
        part_left = lax.dynamic_slice_in_dim(left_panel, first_row, span_rows, 3)
        part_left = part_left.reshape(slices, 2, row_tiles, TILE, span_rows)
        block_of = (first_row + jnp.arange(span_rows, dtype=jnp.int32)) // TILE
        row_weights = jnp.sum(
            jnp.where(block_of[:, None] == block_ids[None, :], tile_weight[:, :, None, :], 0.0),
            axis=-1,
        )
        scaled = (part_left[:, :, :, None, :, :] * row_weights[None, None, :, :, None, :]).astype(
            jnp.bfloat16
        )
        sub_tiles = tile_weight.shape[1]
        right_tiles = incoming.reshape(slices, 2, span_rows, sub_tiles, TILE)
        products = jnp.einsum(
            "fastik,fbktj->fabstij", scaled, right_tiles, preferred_element_type=jnp.float32
        )
        return jnp.stack(
            [products[:, 0, 0] - products[:, 1, 1], products[:, 0, 1] + products[:, 1, 0]], 1
        )

    empty = jnp.zeros((slices, 2, row_tiles, col_tiles, TILE, TILE), jnp.float32)
    incoming = lax.all_gather(recorded, "src", axis=2, tiled=True)
    extent = incoming.shape[2]

    def add_block(first_row, span_rows, running):
        portion = lax.dynamic_slice_in_dim(incoming, first_row, span_rows, 2)
        return running + block_terms(portion, first_row, span_rows, weights)

    sweeps = extent // TILE
    summed = lax.fori_loop(
        0, sweeps, lambda number, running: add_block(number * TILE, TILE, running), empty
    )
    return summed.transpose(0, 1, 2, 4, 3, 5).reshape(slices, 2, own_rows, own_cols)


def solution(mesh):
    in_specs = (P("grp", None, "src", "rcv"), P(("grp", "src"), "rcv", None))
    out_specs = P("grp", None, "src", "rcv")
    return jax.shard_map(shards, mesh=mesh, in_specs=in_specs, out_specs=out_specs, check_vma=False)
```

profile of v0, /device:TPU:1, one launch (start us, length us, event | category | flops | bytes accessed | tf_op | source)
XLA Modules:
  0.0 312.6 jit_solution(3568070417147690657)
XLA Ops:
  7.3 2.0 copy.15
  10.1 63.1 %all-gather.5.cloned.1.call-done = bf16[1,2,256,4096]{3,2,1,0:T(8,128)(2,1)} async-done(((bf16[1,2,256,512]{3,2,1,0:T(8,128)(2,1)}), bf16[1,2,256,4096]{3,2,1,0:T(8,128)(2,1)}) %all-gather.5.cloned.1.call-update) | async-done | bytes 4194320 | tf_op jit(solution)/shard_map/all_gather | solution.py:30
  73.2 131.2 %all-gather.3.cloned.1.call-done = bf16[1,2,4096,512]{2,3,1,0:T(8,128)(2,1)} async-done(((bf16[1,2,256,512]{2,3,1,0:T(8,128)(2,1)}), bf16[1,2,4096,512]{2,3,1,0:T(8,128)(2,1)}) %all-gather.3.cloned.1.call-update) | async-done | bytes 8388624 | tf_op jit(solution)/shard_map/all_gather | solution.py:53
  204.4 99.5 %while.16 = (s32[]{:T(128)}, f32[1,2,2,4,128,128]{4,5,2,3,1,0:T(8,128)S(1)}, bf16[1,2,4096,512]{2,3,1,0:T(8,128)(2,1)}, bf16[1,2,256,4096]{3,2,1,0:T(8,128)(2,1)...) while((s32[]{:T(128)}, ...), condition=%wide.region_2.3_spmd.clone, body=%wide.region_0.2_spmd.clone.sunk | while | flops 135929600 | bytes 10120505 | solution.py:61
  205.4 1.0 constant_dynamic-slice_fusion.5
  207.5 0.9 constant_dynamic-slice_fusion.4
  208.5 1.0 constant_dynamic-slice_fusion.5
  210.6 0.9 constant_dynamic-slice_fusion.4
  211.6 1.0 constant_dynamic-slice_fusion.5
  213.7 0.9 constant_dynamic-slice_fusion.4
  214.7 1.0 constant_dynamic-slice_fusion.5
  216.8 0.9 constant_dynamic-slice_fusion.4
  217.8 1.0 constant_dynamic-slice_fusion.5
  220.0 0.9 constant_dynamic-slice_fusion.4
  220.9 1.0 constant_dynamic-slice_fusion.5
  223.1 0.9 constant_dynamic-slice_fusion.4
  224.0 1.0 constant_dynamic-slice_fusion.5
  226.2 0.9 constant_dynamic-slice_fusion.4
  227.1 1.0 constant_dynamic-slice_fusion.5
  230.2 1.0 constant_dynamic-slice_fusion.5
  232.4 0.9 constant_dynamic-slice_fusion.4
  233.4 1.0 constant_dynamic-slice_fusion.5
  236.5 1.0 constant_dynamic-slice_fusion.5
  239.6 1.0 constant_dynamic-slice_fusion.5
  242.7 1.0 constant_dynamic-slice_fusion.5
  245.8 1.0 constant_dynamic-slice_fusion.5
  248.0 0.9 constant_dynamic-slice_fusion.4
  248.9 1.0 constant_dynamic-slice_fusion.5
  252.0 1.0 constant_dynamic-slice_fusion.5
  254.2 0.9 constant_dynamic-slice_fusion.4
  255.1 1.0 constant_dynamic-slice_fusion.5
  257.3 0.9 constant_dynamic-slice_fusion.4
  258.3 1.0 constant_dynamic-slice_fusion.5
  261.4 1.0 constant_dynamic-slice_fusion.5
  264.5 1.0 constant_dynamic-slice_fusion.5
  267.6 1.0 constant_dynamic-slice_fusion.5
  270.7 1.0 constant_dynamic-slice_fusion.5
  273.8 1.0 constant_dynamic-slice_fusion.5
  276.9 1.0 constant_dynamic-slice_fusion.5
  280.0 1.0 constant_dynamic-slice_fusion.5
  283.1 1.0 constant_dynamic-slice_fusion.5
  286.3 1.0 constant_dynamic-slice_fusion.5
  289.4 1.0 constant_dynamic-slice_fusion.5
  292.5 1.0 constant_dynamic-slice_fusion.5
  295.6 1.0 constant_dynamic-slice_fusion.5
  298.7 1.0 constant_dynamic-slice_fusion.5
  301.8 1.0 constant_dynamic-slice_fusion.5
  304.4 1.4 reshape.136
  (348 shorter events, 57.1 us)
Async XLA Ops:
  6.5 66.7 %all-gather.5.cloned.1.call-start = ((), (), s32[]{:S(2)}) async-start(), calls=%async_computation.1 | async-start | bytes 4718592 | tf_op jit(solution)/shard_map/all_gather | solution.py:30
  7.3 197.1 %all-gather.3.cloned.1.call-start = ((), (), s32[]{:S(2)}) async-start(), calls=%async_computation | async-start | bytes 8912896 | tf_op jit(solution)/shard_map/all_gather | solution.py:53
Sparse Core Ops, SparseCore 0:
  9.4 63.7 all-gather.4
  76.2 128.1 all-gather.2
where the time goes:
time: 314 us; the launch traced here: 313 us
  waiting for transfers between devices  195 us (62%)
  local copies, waits for them, and re-layouts  64.6 us (21%)
  other arithmetic  22.6 us (7%)
  matrix products  13.9 us (4%)
  between operations  13.4 us (4%)
    all_gather x1, waiting for transfers between devices, shards(): incoming = lax.all_gather(recorded, 'src', axis=2, tiled=True)  131 us
    all_gather x1, waiting for transfers between devices, shards(): left_panel = lax.all_gather(recorded, 'rcv', axis=3, tiled=True)  63.1 us
    dynamic_slice x32, local copies, waits for them, and re-layouts, add_block(): portion = lax.dynamic_slice_in_dim(incoming, first_row, span_rows, 2)  31.2 us
    dynamic_slice x32, local copies, waits for them, and re-layouts, block_terms(): part_left = lax.dynamic_slice_in_dim(left_panel, first_row, span_rows, 3)  29.4 us
    dot_general x32, matrix products, block_terms(): jnp.einsum('fastik,fbktj->fabstij', scaled, right_tiles, preferred_elemen...  13.9 us
    add x32, other arithmetic, add_block(): return running + block_terms(portion, first_row, span_rows, weights)  10.7 us
  transfers between devices with their start and end apart: 2, of which 2 were waited for; matrix products, arithmetic and copies ran while one was open for 1% of the time, Pallas kernels for 0%

commit v1 on v0

--- a/solution.py
+++ b/solution.py
@@ -27,7 +27,31 @@
     col_tiles = own_cols // TILE
     weights = tile_weights(aperture)
     block_ids = jnp.arange(NB, dtype=jnp.int32)
-    left_panel = lax.all_gather(recorded, "rcv", axis=3, tiled=True)
+    r2 = jax.lax.axis_size("rcv")
+    top = jax.lax.axis_index("rcv")
+    e_next, newest, block_out = (r2, top, recorded.shape[3])
+    shelf = []
+    for kk in range(e_next):
+        shelf.append((kk, (kk + 1) % e_next))
+    blocks_here = []
+    for kk in range(e_next):
+        blocks_here.append((kk, (kk - 1) % e_next))
+    left_panel = jnp.zeros(
+        (*recorded.shape[:3], e_next * block_out, *recorded.shape[4:]), recorded.dtype
+    )
+    left_panel = lax.dynamic_update_slice_in_dim(left_panel, recorded, newest * block_out, axis=3)
+    current_value = local_part = recorded
+    outer = e_next // 2
+    for dev_i in range(1, outer + 1):
+        current_value = jax.lax.ppermute(current_value, "rcv", shelf)
+        left_panel = lax.dynamic_update_slice_in_dim(
+            left_panel, current_value, (newest - dev_i) % e_next * block_out, axis=3
+        )
+        if dev_i < e_next - outer:
+            local_part = jax.lax.ppermute(local_part, "rcv", perm=blocks_here)
+            left_panel = lax.dynamic_update_slice_in_dim(
+                left_panel, local_part, (newest + dev_i) % e_next * block_out, axis=3
+            )
 
     def block_terms(incoming, first_row, span_rows, tile_weight):
         part_left = lax.dynamic_slice_in_dim(left_panel, first_row, span_rows, 3)

time: 314 us -> 256 us (0.82)
  waiting for transfers between devices: 195 us -> 98.1 us
  starting transfers between devices: 0.04 us -> 28.4 us
  local copies, waits for them, and re-layouts: 64.6 us -> 75.2 us
    all_gather x1 -> x0, waiting for transfers between devices: 63.1 us -> none  [shards(): left_panel = lax.all_gather(recorded, 'rcv', axis=3, tiled=True)]
    all_gather x1, waiting for transfers between devices: 131 us -> 69.5 us  [shards(): incoming = lax.all_gather(recorded, 'src', axis=2, tiled=True)]
    ppermute x0 -> x7, waiting for transfers between devices: none -> 28.6 us  [the longest x4 28.6 us: shards(): current_value = jax.lax.ppermute(current_value, 'rcv', shelf)]
    ppermute x0 -> x7, starting transfers between devices: none -> 28.4 us  [the longest x3 17.8 us: shards(): local_part = jax.lax.ppermute(local_part, 'rcv', perm=blocks_here)]
    dynamic_update_slice x0 -> x8, local copies, waits for them, and re-layouts: none -> 8.05 us  [the longest x4 4.63 us: shards(): lax.dynamic_update_slice_in_dim(left_panel, current_value, (newest - dev_...]
  transfers between devices with their start and end apart: 2 -> 8, of which waited for: 2 -> 5; matrix products, arithmetic and copies ran while one was open for 1% -> 4% of each run, Pallas kernels for 0% -> 0%
where the time goes in v1:
time: 256 us; the launch traced here: 254 us
  waiting for transfers between devices  98.1 us (38%)
  local copies, waits for them, and re-layouts  75.2 us (29%)
  starting transfers between devices  28.4 us (11%)
  other arithmetic  21.9 us (9%)
  matrix products  13.9 us (5%)
  between operations  13.7 us (5%)
  loops' own time  2.99 us (1%)
    all_gather x1, waiting for transfers between devices, shards(): incoming = lax.all_gather(recorded, 'src', axis=2, tiled=True)  69.5 us
    dynamic_slice x32, local copies, waits for them, and re-layouts, add_block(): portion = lax.dynamic_slice_in_dim(incoming, first_row, span_rows, 2)  31.2 us
    dynamic_slice x32, local copies, waits for them, and re-layouts, block_terms(): part_left = lax.dynamic_slice_in_dim(left_panel, first_row, span_rows, 3)  29.4 us
    ppermute x4, waiting for transfers between devices, shards(): current_value = jax.lax.ppermute(current_value, 'rcv', shelf)  28.6 us
    ppermute x3, starting transfers between devices, shards(): local_part = jax.lax.ppermute(local_part, 'rcv', perm=blocks_here)  17.8 us
    dot_general x32, matrix products, block_terms(): jnp.einsum('fastik,fbktj->fabstij', scaled, right_tiles, preferred_elemen...  13.9 us
    add x32, other arithmetic, add_block(): return running + block_terms(portion, first_row, span_rows, weights)  10.7 us
    ppermute x4, starting transfers between devices, shards(): current_value = jax.lax.ppermute(current_value, 'rcv', shelf)  10.6 us
  transfers between devices with their start and end apart: 8, of which 5 were waited for; matrix products, arithmetic and copies ran while one was open for 4% of the time, Pallas kernels for 0%

profile of v1, /device:TPU:1, one launch (start us, length us, event | category | flops | bytes accessed | tf_op | source)
XLA Modules:
  0.0 254.2 jit_solution(6221283350488418075)
XLA Ops:
  6.5 2.1 copy.15
  8.7 4.8 %collective-permute-start = (bf16[1,2,256,512]{3,2,1,0:T(8,128)(2,1)}, bf16[1,2,256,512]{3,2,1,0:T(8,128)(2,1)S(1)}, u32[]{:S(2)}, u32[]{:S(2)}) collective-permute-start(bf16[1,2,256,512]{3,2,1,0:T(8,128)(2,1)} %param.4), channel_id=1, source_target_pairs={{0,1},{1,2},{2,3},{3,4},{4,5},{5,6},{6,7},{7,0},{8,9},{9,10},{10,1... | collective-permute-start | bytes 1572872 | tf_op jit(solution)/shard_map/ppermute | solution.py:46
  13.5 8.6 %collective-permute-start.1 = (bf16[1,2,256,512]{3,2,1,0:T(8,128)(2,1)}, bf16[1,2,256,512]{3,2,1,0:T(8,128)(2,1)S(1)}, u32[]{:S(2)}, u32[]{:S(2)}) collective-permute-start(bf16[1,2,256,512]{3,2,1,0:T(8,128)(2,1)} %param.4), channel_id=1, source_target_pairs={{0,7},{1,0},{2,1},{3,2},{4,3},{5,4},{6,5},{7,6},{8,15},{9,8},{10,9... | collective-permute-start | bytes 1572872 | tf_op jit(solution)/shard_map/ppermute | solution.py:51
  22.1 9.9 %collective-permute-done = bf16[1,2,256,512]{3,2,1,0:T(8,128)(2,1)S(1)} collective-permute-done((bf16[1,2,256,512]{3,2,1,0:T(8,128)(2,1)}, bf16[1,2,256,512]{3,2,1,0:T(8,128)(2,1)S(1)}, u32[]{:S(2)}, u32[]{:S(2)}) %collective-permute-start) | collective-permute-done | bytes 524320 | tf_op jit(solution)/shard_map/ppermute | solution.py:46
  32.0 1.9 collective-permute-start.2
  34.0 4.6 %collective-permute-start.3 = (bf16[1,2,256,512]{3,2,1,0:T(8,128)(2,1)S(1)}, bf16[1,2,256,512]{3,2,1,0:T(8,128)(2,1)S(1)}, u32[]{:S(2)}, u32[]{:S(2)}) collective-permute-start(bf16[1,2,256,512]{3,2,1,0:T(8,128)(2,1)S(1)} %collective-permute-done.1), channel_id=1, source_target_pairs={{0,7},{1,0},{2,1},{3,2},{4,3},{5,4},{6,5},{7,6},{8,15},{9,8},{10,9... | collective-permute-start | bytes 1572872 | tf_op jit(solution)/shard_map/ppermute | solution.py:51
  38.5 8.9 %collective-permute-done.2 = bf16[1,2,256,512]{3,2,1,0:T(8,128)(2,1)} collective-permute-done((bf16[1,2,256,512]{3,2,1,0:T(8,128)(2,1)S(1)}, bf16[1,2,256,512]{3,2,1,0:T(8,128)(2,1)}, u32[]{:S(2)}, u32[]{:S(2)}) %collective-permute-start.2) | collective-permute-done | bytes 524320 | tf_op jit(solution)/shard_map/ppermute | solution.py:46
  47.4 1.9 collective-permute-start.4
  49.5 2.5 broadcast_in_dim.65
  52.9 4.6 %collective-permute-start.5 = (bf16[1,2,256,512]{3,2,1,0:T(8,128)(2,1)S(1)}, bf16[1,2,256,512]{3,2,1,0:T(8,128)(2,1)S(1)}, u32[]{:S(2)}, u32[]{:S(2)}) collective-permute-start(bf16[1,2,256,512]{3,2,1,0:T(8,128)(2,1)S(1)} %collective-permute-done.3), channel_id=1, source_target_pairs={{0,7},{1,0},{2,1},{3,2},{4,3},{5,4},{6,5},{7,6},{8,15},{9,8},{10,9... | collective-permute-start | bytes 1572872 | tf_op jit(solution)/shard_map/ppermute | solution.py:51
  58.5 3.5 %collective-permute-done.4 = bf16[1,2,256,512]{3,2,1,0:T(8,128)(2,1)S(1)} collective-permute-done((bf16[1,2,256,512]{3,2,1,0:T(8,128)(2,1)}, bf16[1,2,256,512]{3,2,1,0:T(8,128)(2,1)S(1)}, u32[]{:S(2)}, u32[]{:S(2)}) %collective-permute-start.4) | collective-permute-done | bytes 524320 | tf_op jit(solution)/shard_map/ppermute | solution.py:46
  62.0 1.9 collective-permute-start.6
  64.8 1.9 constant_dynamic-update-slice_fusion.4
  69.3 6.2 %collective-permute-done.6 = bf16[1,2,256,512]{3,2,1,0:T(8,128)(2,1)S(1)} collective-permute-done((bf16[1,2,256,512]{3,2,1,0:T(8,128)(2,1)S(1)}, bf16[1,2,256,512]{3,2,1,0:T(8,128)(2,1)S(1)}, u32[]{:S(2)}, u32[]{:S(2)}) %collective-permute-start.6) | collective-permute-done | bytes 524320 | tf_op jit(solution)/shard_map/ppermute | solution.py:46
  76.4 69.5 %all-gather.2.cloned.1.call-done = bf16[1,2,4096,512]{2,3,1,0:T(8,128)(2,1)} async-done(((bf16[1,2,256,512]{2,3,1,0:T(8,128)(2,1)}), bf16[1,2,4096,512]{2,3,1,0:T(8,128)(2,1)}) %all-gather.2.cloned.1.call-update) | async-done | bytes 8388624 | tf_op jit(solution)/shard_map/all_gather | solution.py:77
  146.0 99.6 %while.16 = (s32[]{:T(128)}, f32[1,2,2,4,128,128]{4,5,2,3,1,0:T(8,128)S(1)}, bf16[1,2,4096,512]{2,3,1,0:T(8,128)(2,1)}, bf16[1,2,256,4096]{3,2,1,0:T(8,128)(2,1)...) while((s32[]{:T(128)}, ...), condition=%wide.region_2.3_spmd.clone, body=%wide.region_0.2_spmd.clone.sunk | while | flops 135929600 | bytes 10120505 | solution.py:85
  146.9 1.0 constant_dynamic-slice_fusion.5
  150.0 1.0 constant_dynamic-slice_fusion.5
  153.1 1.0 constant_dynamic-slice_fusion.5
  156.3 1.0 constant_dynamic-slice_fusion.5
  159.4 1.0 constant_dynamic-slice_fusion.5
  162.5 1.0 constant_dynamic-slice_fusion.5
  165.6 1.0 constant_dynamic-slice_fusion.5
  168.7 1.0 constant_dynamic-slice_fusion.5
  171.8 1.0 constant_dynamic-slice_fusion.5
  174.9 1.0 constant_dynamic-slice_fusion.5
  178.0 1.0 constant_dynamic-slice_fusion.5
  181.1 1.0 constant_dynamic-slice_fusion.5
  184.3 1.0 constant_dynamic-slice_fusion.5
  187.4 1.0 constant_dynamic-slice_fusion.5
  190.5 1.0 constant_dynamic-slice_fusion.5
  193.6 1.0 constant_dynamic-slice_fusion.5
  196.7 1.0 constant_dynamic-slice_fusion.5
  199.8 1.0 constant_dynamic-slice_fusion.5
  202.9 1.0 constant_dynamic-slice_fusion.5
  206.0 1.0 constant_dynamic-slice_fusion.5
  209.2 1.0 constant_dynamic-slice_fusion.5
  212.3 1.0 constant_dynamic-slice_fusion.5
  215.4 1.0 constant_dynamic-slice_fusion.5
  218.5 1.0 constant_dynamic-slice_fusion.5
  221.6 1.0 constant_dynamic-slice_fusion.5
  224.7 1.0 constant_dynamic-slice_fusion.5
  227.8 1.0 constant_dynamic-slice_fusion.5
  230.9 1.0 constant_dynamic-slice_fusion.5
  237.2 1.0 constant_dynamic-slice_fusion.5
  240.3 1.0 constant_dynamic-slice_fusion.5
  243.4 1.0 constant_dynamic-slice_fusion.5
  245.9 1.4 reshape.136
  (376 shorter events, 72.9 us)
Async XLA Ops:
  6.5 45.5 %copy-start = (bf16[1,2,256,512]{3,2,1,0:T(8,128)(2,1)S(1)}, bf16[1,2,256,512]{3,2,1,0:T(8,128)(2,1)}, u32[]{:S(2)}) copy-start(bf16[1,2,256,512]{3,2,1,0:T(8,128)(2,1)} %param.4) | copy-start | bytes 1572868
  6.5 46.3 %copy-start.3 = (s32[2,4,3]{1,0,2:T(2,128)S(1)}, s32[2,4,3]{1,0,2:T(2,128)}, u32[]{:S(2)}) copy-start(s32[2,4,3]{1,0,2:T(2,128)} %param.5) | copy-start | bytes 292
  6.5 139.4 %all-gather.2.cloned.1.call-start = ((), (), s32[]{:S(2)}) async-start(), calls=%async_computation | async-start | bytes 8912896 | tf_op jit(solution)/shard_map/all_gather | solution.py:77
  8.7 23.4 %collective-permute-start = (bf16[1,2,256,512]{3,2,1,0:T(8,128)(2,1)}, bf16[1,2,256,512]{3,2,1,0:T(8,128)(2,1)S(1)}, u32[]{:S(2)}, u32[]{:S(2)}) collective-permute-start(bf16[1,2,256,512]{3,2,1,0:T(8,128)(2,1)} %param.4), channel_id=1, source_target_pairs={{0,1},{1,2},{2,3},{3,4},{4,5},{5,6},{6,7},{7,0},{8,9},{9,10},{10,1... | collective-permute-start | bytes 1572872 | tf_op jit(solution)/shard_map/ppermute | solution.py:46
  13.5 20.4 %collective-permute-start.1 = (bf16[1,2,256,512]{3,2,1,0:T(8,128)(2,1)}, bf16[1,2,256,512]{3,2,1,0:T(8,128)(2,1)S(1)}, u32[]{:S(2)}, u32[]{:S(2)}) collective-permute-start(bf16[1,2,256,512]{3,2,1,0:T(8,128)(2,1)} %param.4), channel_id=1, source_target_pairs={{0,7},{1,0},{2,1},{3,2},{4,3},{5,4},{6,5},{7,6},{8,15},{9,8},{10,9... | collective-permute-start | bytes 1572872 | tf_op jit(solution)/shard_map/ppermute | solution.py:51
  32.0 17.4 %copy-start.1 = (bf16[1,2,256,512]{3,2,1,0:T(8,128)(2,1)}, bf16[1,2,256,512]{3,2,1,0:T(8,128)(2,1)S(1)}, u32[]{:S(2)}) copy-start(bf16[1,2,256,512]{3,2,1,0:T(8,128)(2,1)S(1)} %collective-permute-done) | copy-start | bytes 1572868
  32.0 15.4 %collective-permute-start.2 = (bf16[1,2,256,512]{3,2,1,0:T(8,128)(2,1)S(1)}, bf16[1,2,256,512]{3,2,1,0:T(8,128)(2,1)}, u32[]{:S(2)}, u32[]{:S(2)}) collective-permute-start(bf16[1,2,256,512]{3,2,1,0:T(8,128)(2,1)S(1)} %collective-permute-done), channel_id=1, source_target_pairs={{0,1},{1,2},{2,3},{3,4},{4,5},{5,6},{6,7},{7,0},{8,9},{9,10},{10,1... | collective-permute-start | bytes 1572872 | tf_op jit(solution)/shard_map/ppermute | solution.py:46
  34.0 18.9 %collective-permute-start.3 = (bf16[1,2,256,512]{3,2,1,0:T(8,128)(2,1)S(1)}, bf16[1,2,256,512]{3,2,1,0:T(8,128)(2,1)S(1)}, u32[]{:S(2)}, u32[]{:S(2)}) collective-permute-start(bf16[1,2,256,512]{3,2,1,0:T(8,128)(2,1)S(1)} %collective-permute-done.1), channel_id=1, source_target_pairs={{0,7},{1,0},{2,1},{3,2},{4,3},{5,4},{6,5},{7,6},{8,15},{9,8},{10,9... | collective-permute-start | bytes 1572872 | tf_op jit(solution)/shard_map/ppermute | solution.py:51
  47.4 14.6 %collective-permute-start.4 = (bf16[1,2,256,512]{3,2,1,0:T(8,128)(2,1)}, bf16[1,2,256,512]{3,2,1,0:T(8,128)(2,1)S(1)}, u32[]{:S(2)}, u32[]{:S(2)}) collective-permute-start(bf16[1,2,256,512]{3,2,1,0:T(8,128)(2,1)} %collective-permute-done.2), channel_id=1, source_target_pairs={{0,1},{1,2},{2,3},{3,4},{4,5},{5,6},{6,7},{7,0},{8,9},{9,10},{10,1... | collective-permute-start | bytes 1572872 | tf_op jit(solution)/shard_map/ppermute | solution.py:46
  49.5 8.0 %copy-start.2 = (bf16[1,2,256,512]{3,2,1,0:T(8,128)(2,1)S(1)}, bf16[1,2,256,512]{3,2,1,0:T(8,128)(2,1)}, u32[]{:S(2)}) copy-start(bf16[1,2,256,512]{3,2,1,0:T(8,128)(2,1)} %copy-done.1) | copy-start | bytes 1572868
  52.9 15.6 %collective-permute-start.5 = (bf16[1,2,256,512]{3,2,1,0:T(8,128)(2,1)S(1)}, bf16[1,2,256,512]{3,2,1,0:T(8,128)(2,1)S(1)}, u32[]{:S(2)}, u32[]{:S(2)}) collective-permute-start(bf16[1,2,256,512]{3,2,1,0:T(8,128)(2,1)S(1)} %collective-permute-done.3), channel_id=1, source_target_pairs={{0,7},{1,0},{2,1},{3,2},{4,3},{5,4},{6,5},{7,6},{8,15},{9,8},{10,9... | collective-permute-start | bytes 1572872 | tf_op jit(solution)/shard_map/ppermute | solution.py:51
  62.0 13.5 %collective-permute-start.6 = (bf16[1,2,256,512]{3,2,1,0:T(8,128)(2,1)S(1)}, bf16[1,2,256,512]{3,2,1,0:T(8,128)(2,1)S(1)}, u32[]{:S(2)}, u32[]{:S(2)}) collective-permute-start(bf16[1,2,256,512]{3,2,1,0:T(8,128)(2,1)S(1)} %collective-permute-done.4), channel_id=1, source_target_pairs={{0,1},{1,2},{2,3},{3,4},{4,5},{5,6},{6,7},{7,0},{8,9},{9,10},{10,1... | collective-permute-start | bytes 1572872 | tf_op jit(solution)/shard_map/ppermute | solution.py:46
Sparse Core Ops, SparseCore 0:
  10.3 135.5 all-gather.1
